TPU v7x, 32 devices: a whole 2x2x4 slice. The times are simulated.
32 devices in a mesh: dp: 16 (over z, y, core), mp: 2 (over x).
Axes of the slice: x: 2, y: 2, z: 4, core: 2. Of those that a mesh axis runs over, the one named last changes fastest.
Arguments:
- layer_input: bfloat16 [24576, 768], P(('dp', 'mp')), may hold values from -6 to 6
- gain_attn: bfloat16 [768], replicated, may hold values from 0.5 to 1.5
- w_query: bfloat16 [768, 768], P(None, 'mp'), may hold values from -0.3125 to 0.3125
- w_key: bfloat16 [768, 768], P(None, 'mp'), may hold values from -0.21875 to 0.21875
- w_value: bfloat16 [768, 768], P(None, 'mp'), may hold values from -0.21875 to 0.21875
- w_out: bfloat16 [768, 768], P('mp'), may hold values from -0.875 to 0.875
- gain_mlp: bfloat16 [768], replicated, may hold values from 0.5 to 1.5
- w_gate: bfloat16 [768, 2048], P(None, 'mp'), may hold values from -0.21875 to 0.21875
- w_up: bfloat16 [768, 2048], P(None, 'mp'), may hold values from -0.21875 to 0.21875
- w_down: bfloat16 [2048, 768], P('mp'), may hold values from -0.125 to 0.125
- segment_start: int32 [16, 7], P('dp'), may hold values from 0 to 1472, as said below
- segment_parent: int32 [16, 7], P('dp'), may hold values from 0 to 2, as said below
- out_grad: bfloat16 [24576, 768], P(('dp', 'mp')), may hold values from -6 to 6
Outputs:
- output: float32 [24576, 768], P(('dp', 'mp'))
- input_grad: float32 [24576, 768], P(('dp', 'mp'))
- gain_attn_grad: float32 [768], replicated
- w_query_grad: float32 [768, 768], P(None, 'mp')
- w_key_grad: float32 [768, 768], P(None, 'mp')
- w_value_grad: float32 [768, 768], P(None, 'mp')
- w_out_grad: float32 [768, 768], P('mp')
- gain_mlp_grad: float32 [768], replicated
- w_gate_grad: float32 [768, 2048], P(None, 'mp')
- w_up_grad: float32 [768, 2048], P(None, 'mp')
- w_down_grad: float32 [2048, 768], P('mp')
Inputs may be any that keep to these rules, and one draw needn't show every extreme that they name: `segment_start`: per tree the segments are stored in order trunk, two branches, four leaves; starts rise strictly from 0, every branch or leaf has 64 to 192 tokens, and the last leaf has exactly 64. `segment_parent`: segment 0 is the trunk (entry 0), segments 1 and 2 have parent 0, and each of them is the parent of exactly two of segments 3 to 6.
All inputs are finite; a program needn't handle non-finite values.
Results may differ from a plain program's by a relative error of at most 0.018.
Values may be sent and summed in bfloat16 or wider, within the bound.
A program may use at most 192 MiB of HBM per device.

v0:
```python
import jax
import jax.numpy as jnp
from jax import lax
from jax.sharding import PartitionSpec as P

HD = 64
EPSILON = 1e-05
ROPE_BASE = 10000.0


def tree_tables(starts, parents, length):
    seg_count = starts.shape[0]
    tok_index = jnp.arange(length, dtype=jnp.int32)
    labels = jnp.arange(seg_count, dtype=jnp.int32)
    segment = jnp.sum(
        (tok_index[:, None] >= starts[None, 1:]).astype(jnp.int32), axis=1, dtype=jnp.int32
    )
    seg_ends = jnp.concatenate([starts[1:], jnp.full((1,), length, dtype=jnp.int32)])
    seg_lengths = seg_ends - starts
    same_seg = (labels[:, None] == labels[None, :]).astype(jnp.int32)
    parent_hot = (parents[:, None] == labels[None, :]).astype(jnp.int32)
    reaches = same_seg + parent_hot + jnp.dot(parent_hot, parent_hot)
    ancestry = (reaches > 0).astype(jnp.int32)
    offset = jnp.dot(ancestry * (1 - same_seg), seg_lengths)
    onehot = (segment[:, None] == labels[None, :]).astype(jnp.int32)
    position = tok_index - jnp.dot(onehot, starts) + jnp.dot(onehot, offset)
    visible = jnp.dot(onehot, ancestry)
    return (position, visible, onehot)


def rotary_tables(position, head_size):
    half_size = head_size // 2
    inv_freq = ROPE_BASE ** (-2.0 * jnp.arange(half_size, dtype=jnp.float32) / head_size)
    angles = position.astype(jnp.float32)[:, None] * inv_freq[None, :]
    return (jnp.cos(angles), jnp.sin(angles))


def rotate(vectors, cosine, sine_tab):
    half_size = vectors.shape[-1] // 2
    first_half = vectors[..., :half_size]
    second = vectors[..., half_size:]
    cos_b = cosine[:, None, :]
    sin_b = sine_tab[:, None, :]
    return jnp.concatenate(
        [first_half * cos_b - second * sin_b, second * cos_b + first_half * sin_b], axis=-1
    )


def rotate_back(gradient, cosine, sine_tab):
    half_size = gradient.shape[-1] // 2
    first_half = gradient[..., :half_size]
    second = gradient[..., half_size:]
    cos_b = cosine[:, None, :]
    sin_b = sine_tab[:, None, :]
    return jnp.concatenate(
        [first_half * cos_b + second * sin_b, second * cos_b - first_half * sin_b], axis=-1
    )


def contract_last(left_mat, right_mat):
    return lax.dot_general(
        left_mat, right_mat, (((1,), (1,)), ((), ())), preferred_element_type=jnp.float32
    )


def inner_rows(left_mat, right_mat):
    return lax.dot_general(
        left_mat, right_mat, (((0,), (0,)), ((), ())), preferred_element_type=jnp.float32
    )


def rms_scale(vectors):
    return lax.rsqrt(jnp.mean(vectors * vectors, axis=-1, keepdims=True) + EPSILON)


def on_device(
    layer_input,
    gain_attn,
    w_query,
    w_key,
    w_value,
    w_out,
    gain_mlp,
    w_gate,
    w_up,
    w_down,
    segment_start,
    segment_parent,
    out_grad,
):
    tok_rows = layer_input.shape[0]
    tree_len = tok_rows * lax.axis_size("mp")
    local_heads = w_query.shape[1] // HD
    score_scale = HD ** (-0.5)
    position, visible, onehot = tree_tables(segment_start[0], segment_parent[0], tree_len)
    cosine, sine_tab = rotary_tables(position, HD)
    block_rows = min(512, tree_len)
    block_starts = jnp.arange(tree_len // block_rows, dtype=jnp.int32) * block_rows
    key_index = jnp.arange(tree_len, dtype=jnp.int32)

    def block_mask(first_row):
        vis_block = lax.dynamic_slice_in_dim(visible, first_row, block_rows, 0)
        q_index = first_row + jnp.arange(block_rows, dtype=jnp.int32)
        return (jnp.dot(vis_block, onehot.T) > 0) & (key_index[None, :] <= q_index[:, None])

    inputs_f32 = layer_input.astype(jnp.float32)
    inv_one = rms_scale(inputs_f32)
    normed = (inputs_f32 * inv_one * gain_attn).astype(jnp.bfloat16)
    normed_all = lax.all_gather(normed, "mp", axis=0, tiled=True)
    q_pre = jnp.dot(normed_all, w_query, preferred_element_type=jnp.float32)
    k_pre = jnp.dot(normed_all, w_key, preferred_element_type=jnp.float32)
    values = jnp.dot(normed_all, w_value, preferred_element_type=jnp.float32).astype(jnp.bfloat16)
    values = values.reshape(tree_len, local_heads, HD)
    query = rotate(q_pre.reshape(tree_len, local_heads, HD), cosine, sine_tab).astype(jnp.bfloat16)
    key_rot = rotate(k_pre.reshape(tree_len, local_heads, HD), cosine, sine_tab).astype(
        jnp.bfloat16
    )

    def attend(first_row):
        q_block = lax.dynamic_slice_in_dim(query, first_row, block_rows, 0)
        scores = (
            jnp.einsum("qhd,khd->hqk", q_block, key_rot, preferred_element_type=jnp.float32)
            * score_scale
        )
        masked = jnp.where(block_mask(first_row)[None], scores, -1e30)
        row_max = jnp.max(masked, axis=-1, keepdims=True)
        exp_terms = jnp.exp(masked - row_max)
        row_sum = jnp.sum(exp_terms, axis=-1, keepdims=True)
        prob_rows = (exp_terms / row_sum).astype(jnp.bfloat16)
        head_out = jnp.einsum("hqk,khd->qhd", prob_rows, values, preferred_element_type=jnp.float32)
        return (head_out.astype(jnp.bfloat16), row_max[..., 0] + jnp.log(row_sum[..., 0]))

    head_blocks, lse_blocks = lax.map(attend, block_starts)
    heads_out = head_blocks.reshape(tree_len, local_heads * HD)
    attn_out = lax.psum_scatter(
        jnp.dot(heads_out, w_out, preferred_element_type=jnp.float32).astype(jnp.bfloat16),
        "mp",
        scatter_dimension=0,
        tiled=True,
    ).astype(jnp.float32)
    residual = inputs_f32 + attn_out
    inv_two = rms_scale(residual)
    normed_two = (residual * inv_two * gain_mlp).astype(jnp.bfloat16)
    normed_two_all = lax.all_gather(normed_two, "mp", axis=0, tiled=True)
    gate_pre = jnp.dot(normed_two_all, w_gate, preferred_element_type=jnp.float32)
    up_pre = jnp.dot(normed_two_all, w_up, preferred_element_type=jnp.float32)
    sigmoid_gate = jax.nn.sigmoid(gate_pre)
    silu_gate = gate_pre * sigmoid_gate
    hidden = (silu_gate * up_pre).astype(jnp.bfloat16)
    output = residual + lax.psum_scatter(
        jnp.dot(hidden, w_down, preferred_element_type=jnp.float32).astype(jnp.bfloat16),
        "mp",
        scatter_dimension=0,
        tiled=True,
    ).astype(jnp.float32)
    grads_all = lax.all_gather(out_grad, "mp", axis=0, tiled=True)
    grad_down = inner_rows(hidden, grads_all)
    d_hidden = contract_last(grads_all, w_down)
    d_gate = (d_hidden * up_pre * sigmoid_gate * (1.0 + gate_pre * (1.0 - sigmoid_gate))).astype(
        jnp.bfloat16
    )
    d_up = (d_hidden * silu_gate).astype(jnp.bfloat16)
    grad_gate = inner_rows(normed_two_all, d_gate)
    grad_up = inner_rows(normed_two_all, d_up)
    d_norm_two = lax.psum_scatter(
        (contract_last(d_gate, w_gate) + contract_last(d_up, w_up)).astype(jnp.bfloat16),
        "mp",
        scatter_dimension=0,
        tiled=True,
    ).astype(jnp.float32)
    scaled_two = gain_mlp * d_norm_two
    gain_mlp_part = jnp.sum(d_norm_two * residual * inv_two, axis=0)
    d_resid = (
        out_grad.astype(jnp.float32)
        + inv_two * scaled_two
        - residual * inv_two**3 * jnp.mean(scaled_two * residual, axis=-1, keepdims=True)
    )
    d_attn_all = lax.all_gather(d_resid.astype(jnp.bfloat16), "mp", axis=0, tiled=True)
    grad_out = inner_rows(heads_out, d_attn_all)
    d_heads = (
        contract_last(d_attn_all, w_out).astype(jnp.bfloat16).reshape(tree_len, local_heads, HD)
    )

    def attend_back(sums_in, block_items):
        key_acc, value_acc = sums_in
        first_row, lse_block = block_items
        q_block = lax.dynamic_slice_in_dim(query, first_row, block_rows, 0)
        d_block = lax.dynamic_slice_in_dim(d_heads, first_row, block_rows, 0)
        scores = (
            jnp.einsum("qhd,khd->hqk", q_block, key_rot, preferred_element_type=jnp.float32)
            * score_scale
        )
        masked = jnp.where(block_mask(first_row)[None], scores, -1e30)
        prob_rows = jnp.exp(masked - lse_block[..., None])
        d_probs = jnp.einsum("qhd,khd->hqk", d_block, values, preferred_element_type=jnp.float32)
        row_dot = jnp.sum(prob_rows * d_probs, axis=-1, keepdims=True)
        d_scores = (prob_rows * (d_probs - row_dot)).astype(jnp.bfloat16)
        d_query_block = (
            jnp.einsum("hqk,khd->qhd", d_scores, key_rot, preferred_element_type=jnp.float32)
            * score_scale
        )
        key_acc = (
            key_acc
            + jnp.einsum("hqk,qhd->khd", d_scores, q_block, preferred_element_type=jnp.float32)
            * score_scale
        )
        value_acc = value_acc + jnp.einsum(
            "hqk,qhd->khd",
            prob_rows.astype(jnp.bfloat16),
            d_block,
            preferred_element_type=jnp.float32,
        )
        return ((key_acc, value_acc), d_query_block)

    zero_grads = jnp.zeros((tree_len, local_heads, HD), jnp.float32)
    (d_key_rot, d_value_acc), d_query_blocks = lax.scan(
        attend_back, (zero_grads, zero_grads), (block_starts, lse_blocks)
    )
    d_query_rot = d_query_blocks.reshape(tree_len, local_heads, HD)
    d_qpre = (
        rotate_back(d_query_rot, cosine, sine_tab)
        .reshape(tree_len, local_heads * HD)
        .astype(jnp.bfloat16)
    )
    d_kpre = (
        rotate_back(d_key_rot, cosine, sine_tab)
        .reshape(tree_len, local_heads * HD)
        .astype(jnp.bfloat16)
    )
    d_value = d_value_acc.reshape(tree_len, local_heads * HD).astype(jnp.bfloat16)
    grad_query = inner_rows(normed_all, d_qpre)
    grad_key = inner_rows(normed_all, d_kpre)
    grad_value = inner_rows(normed_all, d_value)
    d_norm_one = lax.psum_scatter(
        (
            contract_last(d_qpre, w_query)
            + contract_last(d_kpre, w_key)
            + contract_last(d_value, w_value)
        ).astype(jnp.bfloat16),
        "mp",
        scatter_dimension=0,
        tiled=True,
    ).astype(jnp.float32)
    scaled_one = gain_attn * d_norm_one
    gain_attn_part = jnp.sum(d_norm_one * inputs_f32 * inv_one, axis=0)
    input_grad = (
        d_resid
        + inv_one * scaled_one
        - inputs_f32 * inv_one**3 * jnp.mean(scaled_one * inputs_f32, axis=-1, keepdims=True)
    )
    gain_attn_grad, gain_mlp_grad = lax.psum((gain_attn_part, gain_mlp_part), ("dp", "mp"))
    grad_query, grad_key, grad_value, grad_out, grad_gate, grad_up, grad_down = lax.psum(
        (grad_query, grad_key, grad_value, grad_out, grad_gate, grad_up, grad_down), "dp"
    )
    return (
        output,
        input_grad,
        gain_attn_grad,
        grad_query,
        grad_key,
        grad_value,
        grad_out,
        gain_mlp_grad,
        grad_gate,
        grad_up,
        grad_down,
    )


def solution(mesh):
    in_specs = (
        P(("dp", "mp"), None),
        P(),
        P(None, "mp"),
        P(None, "mp"),
        P(None, "mp"),
        P("mp", None),
        P(),
        P(None, "mp"),
        P(None, "mp"),
        P("mp", None),
        P("dp", None),
        P("dp", None),
        P(("dp", "mp"), None),
    )
    out_specs = (
        P(("dp", "mp"), None),
        P(("dp", "mp"), None),
        P(),
        P(None, "mp"),
        P(None, "mp"),
        P(None, "mp"),
        P("mp", None),
        P(),
        P(None, "mp"),
        P(None, "mp"),
        P("mp", None),
    )
    return jax.shard_map(
        on_device, mesh=mesh, in_specs=in_specs, out_specs=out_specs, check_vma=False
    )
```

profile of v0, /device:TPU:0, one launch (start us, length us, event | category | flops | bytes accessed | tf_op | source)
XLA Modules:
  0.0 983.7 jit_solution(3247048086694837235)
XLA Ops:
  16.7 35.2 %all-gather.5.cloned.1.call-done = bf16[1536,768]{1,0:T(8,128)(2,1)} async-done(((bf16[768,768]{1,0:T(8,128)(2,1)}), bf16[1536,768]{1,0:T(8,128)(2,1)}) %all-gather.5.cloned.1.call-update) | async-done | bytes 2359312 | tf_op jit(solution)/shard_map/all_gather | solution.py:109
  60.2 82.6 %while.28 = (s32[]{:T(128)}, bf16[3,512,6,64]{1,3,2,0:T(8,128)(2,1)}, f32[3,6,512]{2,1,0:T(8,128)}, s32[3]{0:T(128)S(1)}, s32[1536,7]{0,1:T(8,128)}, /*index=5*/...) while((s32[]{:T(128)}, ...), condition=%wide.region_5.6_spmd.clone, body=%wide.region_2.5_spmd.clone.sunk | while | flops 1278167552 | bytes 63043776 | solution.py:133
  63.8 6.4 fusion.192
  79.9 7.5 fusion.195
  107.2 7.5 fusion.195
  134.5 7.5 fusion.195
  150.0 34.2 %reduce-scatter.5.cloned.1.call-done = bf16[768,768]{1,0:T(8,128)(2,1)} async-done(((bf16[1536,768]{1,0:T(8,128)(2,1)}), bf16[768,768]{1,0:T(8,128)(2,1)}) %reduce-scatter.5.cloned.1.call-update) | async-done | bytes 1179664 | tf_op jit(solution)/shard_map/reduce_scatter | solution.py:135
  188.7 35.6 %all-gather.7.cloned.1.call-done = bf16[1536,768]{1,0:T(8,128)(2,1)} async-done(((bf16[768,768]{1,0:T(8,128)(2,1)}), bf16[1536,768]{1,0:T(8,128)(2,1)}) %all-gather.7.cloned.1.call-update) | async-done | bytes 2359312 | tf_op jit(solution)/shard_map/all_gather | solution.py:144
  224.3 7.6 fusion.103
  236.3 25.6 %all-gather.9.cloned.1.call-done = bf16[1536,768]{1,0:T(8,128)(2,1)} async-done(((bf16[768,768]{1,0:T(8,128)(2,1)}), bf16[1536,768]{1,0:T(8,128)(2,1)}) %all-gather.9.cloned.1.call-update) | async-done | bytes 2359312 | tf_op jit(solution)/shard_map/all_gather | solution.py:156
  261.9 10.2 %multiply_convert_fusion.1 = (bf16[1536,1024]{1,0:T(8,128)(2,1)S(1)}, bf16[1536,1024]{1,0:T(8,128)(2,1)S(1)}, bf16[1536,1024]{1,0:T(8,128)(2,1)}) fusion(f32[1536,1024]{1,0:T(8,128)} %fusion.102, f32[1536,1024]{1,0:T(8,128)} %fusion.103, bf16[1536,768]{1,0:T(8,128)(2,1)} %all-gather.9.cloned.1.call-done, bf16[1024,768]{1,0:T(8,128)(2,1)S(1)} %copy-done), kind=kOutput, calls=%fused_computation.61 | convolution fusion | flops 2439512064 | bytes 25952256 | tf_op jit(solution)/shard_map/dot_general | solution.py:61
  278.8 34.8 %reduce-scatter.9.cloned.1.call-done = bf16[768,768]{1,0:T(8,128)(2,1)} async-done(((bf16[1536,768]{1,0:T(8,128)(2,1)}), bf16[768,768]{1,0:T(8,128)(2,1)}) %reduce-scatter.9.cloned.1.call-update) | async-done | bytes 1179664 | tf_op jit(solution)/shard_map/reduce_scatter | solution.py:165
  321.3 36.2 %all-gather.11.cloned.1.call-done = bf16[1536,768]{1,0:T(8,128)(2,1)} async-done(((bf16[768,768]{1,0:T(8,128)(2,1)}), bf16[1536,768]{1,0:T(8,128)(2,1)}) %all-gather.11.cloned.1.call-update) | async-done | bytes 2359312 | tf_op jit(solution)/shard_map/all_gather | solution.py:178
  361.3 243.4 %while.29 = (s32[]{:T(128)}, f32[1536,6,64]{0,2,1:T(8,128)}, f32[1536,6,64]{0,2,1:T(8,128)}, f32[3,512,6,64]{1,0,3,2:T(4,128)}, s32[3]{0:T(128)S(1)}, /*index=5*...) while((s32[]{:T(128)}, f32[1536,6,64]{0,2,1:T(8,128)}, ...), condition=%wide.region_13.14_spmd.clone, body=%wide.region_11.13_spmd.clone.sunk | while | flops 3107211776 | bytes 262388048 | solution.py:216
  375.9 6.5 copy-done.1
  382.4 7.8 fusion.210
  390.2 14.7 %multiply_reduce_fusion.3 = (f32[6,512]{1,0:T(8,128)S(1)}, f32[6,512,1536]{2,1,0:T(8,128)}) fusion(f32[6,512,1536]{2,1,0:T(8,128)} %copy-done.1, f32[6,512]{1,0:T(8,128)S(1)} %dynamic-slice_bitcast_fusion.2, pred[512,1536]{1,0:T(8,128)(4,1)S(1)} %fusion.208, bf16[1536,6,64]{0,2,1:T(8,128)(2,1)S(1)} %copy-done.8, ...), kind=kOutput, calls=%fused_computation.28.clone.1 | convolution fusion | flops 627569664 | bytes 40132612 | tf_op jit(solution)/shard_map/while/body/eval_jaxpr/qhd,khd->hqk/dot_general | solution.py:195
  404.8 13.2 %multiply_convert_fusion.6 = bf16[6,512,1536]{2,1,0:T(8,128)(2,1)S(1)} fusion(f32[6,512,1536]{2,1,0:T(8,128)} %get-tuple-element.422, f32[6,512,1536]{2,1,0:T(8,128)} %copy-done.1, f32[6,512]{1,0:T(8,128)S(1)} %get-tuple-element.423, f32[6,512]{1,0:T(8,128)S(1)} %dynamic-slice_bitcast_fusion.2, pred[512,1536]{1,0:T(8,128)(4,1)S(1)} %fusion.208), kind=kLoop, calls=%fused_computation.27.clone.1 | loop fusion | flops 28311552 | bytes 47996928 | tf_op jit(solution)/shard_map/while/body/eval_jaxpr/convert_element_type | solution.py:197
  426.3 16.1 %dynamic_update_slice.22 = f32[3,512,6,64]{1,0,3,2:T(4,128)} dynamic-update-slice(f32[3,512,6,64]{1,0,3,2:T(4,128)} %get-tuple-element.478, f32[1,512,6,64]{1,0,3,2:T(1,128)S(1)} %copy.38, s32[]{:T(128)S(6)} %copy.55, s32[]{:T(128)} %constant.41.clone.1..sunk.1, s32[]{:T(128)} %constant.41.clone.1..sunk.1, s32[]{:T(128)} %constant.41.clone.1..sunk.1) | dynamic-update-slice | bytes 1572868 | tf_op jit(solution)/shard_map/while/body/jit(dynamic_update_index_in_dim)/dynamic_update_slice | solution.py:216
  456.6 6.5 copy-done.1
  463.1 8.2 fusion.210
  471.4 14.6 %multiply_reduce_fusion.3 = (f32[6,512]{1,0:T(8,128)S(1)}, f32[6,512,1536]{2,1,0:T(8,128)}) fusion(f32[6,512,1536]{2,1,0:T(8,128)} %copy-done.1, f32[6,512]{1,0:T(8,128)S(1)} %dynamic-slice_bitcast_fusion.2, pred[512,1536]{1,0:T(8,128)(4,1)S(1)} %fusion.208, bf16[1536,6,64]{0,2,1:T(8,128)(2,1)S(1)} %copy-done.8, ...), kind=kOutput, calls=%fused_computation.28.clone.1 | convolution fusion | flops 627569664 | bytes 40132612 | tf_op jit(solution)/shard_map/while/body/eval_jaxpr/qhd,khd->hqk/dot_general | solution.py:195
  486.0 13.2 %multiply_convert_fusion.6 = bf16[6,512,1536]{2,1,0:T(8,128)(2,1)S(1)} fusion(f32[6,512,1536]{2,1,0:T(8,128)} %get-tuple-element.422, f32[6,512,1536]{2,1,0:T(8,128)} %copy-done.1, f32[6,512]{1,0:T(8,128)S(1)} %get-tuple-element.423, f32[6,512]{1,0:T(8,128)S(1)} %dynamic-slice_bitcast_fusion.2, pred[512,1536]{1,0:T(8,128)(4,1)S(1)} %fusion.208), kind=kLoop, calls=%fused_computation.27.clone.1 | loop fusion | flops 28311552 | bytes 47996928 | tf_op jit(solution)/shard_map/while/body/eval_jaxpr/convert_element_type | solution.py:197
  507.5 16.1 %dynamic_update_slice.22 = f32[3,512,6,64]{1,0,3,2:T(4,128)} dynamic-update-slice(f32[3,512,6,64]{1,0,3,2:T(4,128)} %get-tuple-element.478, f32[1,512,6,64]{1,0,3,2:T(1,128)S(1)} %copy.38, s32[]{:T(128)S(6)} %copy.55, s32[]{:T(128)} %constant.41.clone.1..sunk.1, s32[]{:T(128)} %constant.41.clone.1..sunk.1, s32[]{:T(128)} %constant.41.clone.1..sunk.1) | dynamic-update-slice | bytes 1572868 | tf_op jit(solution)/shard_map/while/body/jit(dynamic_update_index_in_dim)/dynamic_update_slice | solution.py:216
  537.7 6.5 copy-done.1
  544.2 8.2 fusion.210
  552.4 14.6 %multiply_reduce_fusion.3 = (f32[6,512]{1,0:T(8,128)S(1)}, f32[6,512,1536]{2,1,0:T(8,128)}) fusion(f32[6,512,1536]{2,1,0:T(8,128)} %copy-done.1, f32[6,512]{1,0:T(8,128)S(1)} %dynamic-slice_bitcast_fusion.2, pred[512,1536]{1,0:T(8,128)(4,1)S(1)} %fusion.208, bf16[1536,6,64]{0,2,1:T(8,128)(2,1)S(1)} %copy-done.8, ...), kind=kOutput, calls=%fused_computation.28.clone.1 | convolution fusion | flops 627569664 | bytes 40132612 | tf_op jit(solution)/shard_map/while/body/eval_jaxpr/qhd,khd->hqk/dot_general | solution.py:195
  567.0 13.2 %multiply_convert_fusion.6 = bf16[6,512,1536]{2,1,0:T(8,128)(2,1)S(1)} fusion(f32[6,512,1536]{2,1,0:T(8,128)} %get-tuple-element.422, f32[6,512,1536]{2,1,0:T(8,128)} %copy-done.1, f32[6,512]{1,0:T(8,128)S(1)} %get-tuple-element.423, f32[6,512]{1,0:T(8,128)S(1)} %dynamic-slice_bitcast_fusion.2, pred[512,1536]{1,0:T(8,128)(4,1)S(1)} %fusion.208), kind=kLoop, calls=%fused_computation.27.clone.1 | loop fusion | flops 28311552 | bytes 47996928 | tf_op jit(solution)/shard_map/while/body/eval_jaxpr/convert_element_type | solution.py:197
  588.4 16.1 %dynamic_update_slice.22 = f32[3,512,6,64]{1,0,3,2:T(4,128)} dynamic-update-slice(f32[3,512,6,64]{1,0,3,2:T(4,128)} %get-tuple-element.478, f32[1,512,6,64]{1,0,3,2:T(1,128)S(1)} %copy.38, s32[]{:T(128)S(6)} %copy.55, s32[]{:T(128)} %constant.41.clone.1..sunk.1, s32[]{:T(128)} %constant.41.clone.1..sunk.1, s32[]{:T(128)} %constant.41.clone.1..sunk.1) | dynamic-update-slice | bytes 1572868 | tf_op jit(solution)/shard_map/while/body/jit(dynamic_update_index_in_dim)/dynamic_update_slice | solution.py:216
  628.6 7.2 fusion.113
  659.5 39.7 %all-reduce = (f32[768]{0:T(1024)}, f32[768]{0:T(1024)}) all-reduce(f32[768]{0:T(1024)S(1)} %get-tuple-element.206, f32[768]{0:T(1024)S(1)} %copy-done.47), channel_id=1, replica_groups=mesh['dp'=16,'mp'=2] {'dp','mp'}, use_global_device_ids=true, to_apply=%region_17.18 | all-reduce | flops 1536 | bytes 12288 | tf_op jit(solution)/shard_map/psum | solution.py:251
  704.4 258.5 %all-reduce.4.cloned.1.call-done = (f32[768,384]{1,0:T(8,128)}, f32[768,384]{1,0:T(8,128)}, f32[768,384]{1,0:T(8,128)}, f32[384,768]{1,0:T(8,128)}, f32[768,1024...) async-done(((f32[768,384]{1,0:T(8,128)}, f32[768,384]{1,0:T(8,128)}, f32[768,384]{1,0:T(8,128)}, f32[384,768]{1,0:T(8,128)}, f32[768,1024]{1,0:T(8,128)}, ...) | async-done | bytes 14155792 | tf_op jit(solution)/shard_map/psum | solution.py:252
  (265 shorter events, 226.8 us)
Async XLA Ops:
  7.2 254.7 %copy-start = (bf16[1024,768]{1,0:T(8,128)(2,1)S(1)}, bf16[1024,768]{1,0:T(8,128)(2,1)}, u32[]{:S(2)}) copy-start(bf16[1024,768]{1,0:T(8,128)(2,1)} %param.26) | copy-start | bytes 4718596
  7.2 44.7 %all-gather.5.cloned.1.call-start = ((), (), s32[]{:S(2)}) async-start(), calls=%async_computation.4 | async-start | bytes 3538944 | tf_op jit(solution)/shard_map/all_gather | solution.py:109
  10.2 41.6 %copy-start.30 = (bf16[768,384]{1,0:T(8,128)(2,1)S(1)}, bf16[768,384]{1,0:T(8,128)(2,1)}, u32[]{:S(2)}) copy-start(bf16[768,384]{1,0:T(8,128)(2,1)} %param.20) | copy-start | bytes 1769476
  13.0 171.3 %reduce-scatter.5.cloned.1.call-start = ((), (), s32[]{:S(2)}) async-start(), calls=%async_computation.5 | async-start | bytes 3538944 | tf_op jit(solution)/shard_map/reduce_scatter | solution.py:135
  16.7 39.3 %copy-start.19 = (f32[1536,32]{0,1:T(8,128)}, f32[1536,32]{0,1:T(8,128)S(1)}, u32[]{:S(2)}) copy-start(f32[1536,32]{0,1:T(8,128)S(1)} %get-tuple-element.280) | copy-start | bytes 589828
  16.7 39.3 %copy-start.21 = (f32[1536,32]{0,1:T(8,128)}, f32[1536,32]{0,1:T(8,128)S(1)}, u32[]{:S(2)}) copy-start(f32[1536,32]{0,1:T(8,128)S(1)} %get-tuple-element.281) | copy-start | bytes 589828
  16.7 38.1 %copy-start.28 = (bf16[768,384]{1,0:T(8,128)(2,1)S(1)}, bf16[768,384]{1,0:T(8,128)(2,1)}, u32[]{:S(2)}) copy-start(bf16[768,384]{1,0:T(8,128)(2,1)} %param.19) | copy-start | bytes 1769476
  149.4 74.9 %all-gather.7.cloned.1.call-start = ((), (), s32[]{:S(2)}) async-start(), calls=%async_computation.6 | async-start | bytes 3538944 | tf_op jit(solution)/shard_map/all_gather | solution.py:144
  150.0 167.4 %copy-start.34 = (f32[768]{0:T(1024)}, f32[768]{0:T(1024)S(1)}, u32[]{:S(2)}) copy-start(f32[768]{0:T(1024)S(1)} %convert_element_type.122) | copy-start | bytes 9220
  186.5 130.9 %copy-start.36 = (f32[768]{0:T(1024)}, f32[768]{0:T(1024)S(1)}, u32[]{:S(2)}) copy-start(f32[768]{0:T(1024)S(1)} %get-tuple-element.285) | copy-start | bytes 9220
  186.5 130.9 %copy-start.42 = (f32[768]{0:T(1024)}, f32[768]{0:T(1024)S(1)}, u32[]{:S(2)}) copy-start(f32[768]{0:T(1024)S(1)} %get-tuple-element.284) | copy-start | bytes 9220
  188.1 73.8 %all-gather.9.cloned.1.call-start = ((), (), s32[]{:S(2)}) async-start(), calls=%async_computation.8 | async-start | bytes 3538944 | tf_op jit(solution)/shard_map/all_gather | solution.py:156
  188.6 125.0 %reduce-scatter.9.cloned.1.call-start = ((), (), s32[]{:S(2)}) async-start(), calls=%async_computation.9 | async-start | bytes 3538944 | tf_op jit(solution)/shard_map/reduce_scatter | solution.py:165
  224.3 7.6 copy-start.51
  224.3 7.6 copy-start.54
  261.9 10.2 %copy-start.55 = (bf16[768,1024]{1,0:T(8,128)(2,1)S(1)}, bf16[768,1024]{1,0:T(8,128)(2,1)}, u32[]{:S(2)}) copy-start(bf16[768,1024]{1,0:T(8,128)(2,1)} %param.24) | copy-start | bytes 4718596
  278.8 78.7 %all-gather.11.cloned.1.call-start = ((), (), s32[]{:S(2)}) async-start(), calls=%async_computation.10 | async-start | bytes 3538944 | tf_op jit(solution)/shard_map/all_gather | solution.py:178
  321.2 335.9 %reduce-scatter.11.cloned.1.call-start = ((), (), s32[]{:S(2)}) async-start(), calls=%async_computation.11 | async-start | bytes 3538944 | tf_op jit(solution)/shard_map/reduce_scatter | solution.py:234
  382.4 7.8 copy-start.8
  456.6 6.5 copy-start.1
  463.1 8.3 copy-start.8
  544.2 8.2 copy-start.8
  611.5 7.9 copy-start.14
  622.3 77.0 %reduce-scatter.7.cloned.1.call-start = ((), (), s32[]{:S(2)}) async-start(), calls=%async_computation.7 | async-start | bytes 3538944 | tf_op jit(solution)/shard_map/reduce_scatter | solution.py:150
  628.3 334.6 %all-reduce.4.cloned.1.call-start = ((), (), s32[]{:S(2)}) async-start(), calls=%async_computation.12 | async-start | bytes 28311552 | tf_op jit(solution)/shard_map/psum | solution.py:252
  628.5 7.2 copy-start.52
  628.5 7.2 copy-start.63
  654.0 45.3 %copy-start.35 = (f32[768]{0:T(1024)S(1)}, f32[768]{0:T(1024)}, u32[]{:S(2)}) copy-start(f32[768]{0:T(1024)} %copy-done.34) | copy-start | bytes 9220
  654.0 45.3 %copy-start.37 = (f32[768]{0:T(1024)S(1)}, f32[768]{0:T(1024)}, u32[]{:S(2)}) copy-start(f32[768]{0:T(1024)} %copy-done.36) | copy-start | bytes 9220
  654.0 45.3 %copy-start.43 = (f32[768]{0:T(1024)S(1)}, f32[768]{0:T(1024)}, u32[]{:S(2)}) copy-start(f32[768]{0:T(1024)} %copy-done.42) | copy-start | bytes 9220
  654.1 45.3 %copy-start.45 = (f32[768]{0:T(1024)S(1)}, f32[768]{0:T(1024)}, u32[]{:S(2)}) copy-start(f32[768]{0:T(1024)} %copy-done.44) | copy-start | bytes 9220
  654.1 45.3 %copy-start.46 = (f32[768]{0:T(1024)S(1)}, f32[768]{0:T(1024)}, u32[]{:S(2)}) copy-start(f32[768]{0:T(1024)} %get-tuple-element.282) | copy-start | bytes 9220
  (49 other events, 147.8 us)
Sparse Core Ops, SparseCore 0:
  13.1 38.7 all-gather.4
  149.5 34.7 reduce-scatter.4
  188.2 36.0 all-gather.6
  225.8 36.0 all-gather.8
  278.9 34.6 reduce-scatter.8
  321.4 36.0 all-gather.10
  622.4 34.7 reduce-scatter.10
  660.1 35.1 reduce-scatter.6
  701.8 260.9 all-reduce.3
where the time goes:
time: 992 us; the launch traced here: 984 us
  waiting for transfers between devices  464 us (47%)
  matrix products  254 us (26%)
  local copies, waits for them, and re-layouts  107 us (11%)
  other arithmetic  91.1 us (9%)
  blocking collectives  39.7 us (4%)
  between operations  14.7 us (1%)
  loops' own time  13.4 us (1%)
    psum x1, waiting for transfers between devices, on_device(): lax.psum((grad_query, grad_key, grad_value, grad_out, grad_gate, grad_up,...  258 us
    dynamic_update_slice x6, local copies, waits for them, and re-layouts, on_device(): lax.scan(attend_back, (zero_grads, zero_grads), (block_starts, lse_blocks))  50.6 us
    dot_general x3, matrix products, attend_back(): jnp.einsum('qhd,khd->hqk', d_block, values, preferred_element_type=jnp.fl...  43.8 us
    psum x1, blocking collectives, on_device(): lax.psum((gain_attn_part, gain_mlp_part), ('dp', 'mp'))  39.7 us
    convert_element_type x3, other arithmetic, attend_back(): d_scores = (prob_rows * (d_probs - row_dot)).astype(jnp.bfloat16)  39.7 us
    dot_general x6, matrix products, block_mask(): jnp.dot(vis_block, onehot.T) > 0  38.2 us
    all_gather x1, waiting for transfers between devices, on_device(): lax.all_gather(d_resid.astype(jnp.bfloat16), 'mp', axis=0, tiled=True)  36.2 us
    all_gather x1, waiting for transfers between devices, on_device(): normed_two_all = lax.all_gather(normed_two, 'mp', axis=0, tiled=True)  35.6 us
  transfers between devices with their start and end apart: 9, of which 8 were waited for; matrix products, arithmetic and copies ran while one was open for 6% of the time, Pallas kernels for 0%

commit v1 on v0

--- a/solution.py
+++ b/solution.py
@@ -1,11 +1,22 @@
+import functools
 import jax
 import jax.numpy as jnp
 from jax import lax
 from jax.sharding import PartitionSpec as P
+from jax.lax import psum
 
 HD = 64
 EPSILON = 1e-05
 ROPE_BASE = 10000.0
+
+
+def load_target(vector, ax_name, along_axis):
+    for k in (ax_name, along_axis):
+        vector = psum(vector, k)
+    return vector
+
+
+report_the_leaves = functools.partial(load_target, ax_name="dp", along_axis="mp")
 
 
 def tree_tables(starts, parents, length):
@@ -248,7 +259,7 @@
         + inv_one * scaled_one
         - inputs_f32 * inv_one**3 * jnp.mean(scaled_one * inputs_f32, axis=-1, keepdims=True)
     )
-    gain_attn_grad, gain_mlp_grad = lax.psum((gain_attn_part, gain_mlp_part), ("dp", "mp"))
+    gain_attn_grad, gain_mlp_grad = report_the_leaves((gain_attn_part, gain_mlp_part))
     grad_query, grad_key, grad_value, grad_out, grad_gate, grad_up, grad_down = lax.psum(
         (grad_query, grad_key, grad_value, grad_out, grad_gate, grad_up, grad_down), "dp"
     )

time: 992 us -> 992 us (level)
    psum x1 -> x2, blocking collectives: 39.7 us -> 39.3 us  [load_target(): vector = psum(vector, k)]
    while x24 -> x18, local copies, waits for them, and re-layouts: 23.6 us -> 23.6 us
where the time goes in v1:
time: 992 us; the launch traced here: 983 us
  waiting for transfers between devices  464 us (47%)
  matrix products  254 us (26%)
  local copies, waits for them, and re-layouts  107 us (11%)
  other arithmetic  91 us (9%)
  blocking collectives  39.3 us (4%)
  between operations  14.7 us (1%)
  loops' own time  13 us (1%)
    psum x1, waiting for transfers between devices, on_device(): lax.psum((grad_query, grad_key, grad_value, grad_out, grad_gate, grad_up,...  259 us
    dynamic_update_slice x6, local copies, waits for them, and re-layouts, on_device(): lax.scan(attend_back, (zero_grads, zero_grads), (block_starts, lse_blocks))  50.6 us
    dot_general x3, matrix products, attend_back(): jnp.einsum('qhd,khd->hqk', d_block, values, preferred_element_type=jnp.fl...  44.1 us
    convert_element_type x3, other arithmetic, attend_back(): d_scores = (prob_rows * (d_probs - row_dot)).astype(jnp.bfloat16)  39.7 us
    psum x2, blocking collectives, load_target(): vector = psum(vector, k)  39.3 us
    dot_general x6, matrix products, block_mask(): jnp.dot(vis_block, onehot.T) > 0  38.2 us
    all_gather x1, waiting for transfers between devices, on_device(): lax.all_gather(d_resid.astype(jnp.bfloat16), 'mp', axis=0, tiled=True)  36.2 us
    all_gather x1, waiting for transfers between devices, on_device(): normed_two_all = lax.all_gather(normed_two, 'mp', axis=0, tiled=True)  35.6 us
  transfers between devices with their start and end apart: 9, of which 8 were waited for; matrix products, arithmetic and copies ran while one was open for 6% of the time, Pallas kernels for 0%

profile of v1, /device:TPU:0, one launch (start us, length us, event | category | flops | bytes accessed | tf_op | source)
XLA Modules:
  0.0 983.4 jit_solution(17907645116783695451)
XLA Ops:
  17.3 35.2 %all-gather.5.cloned.1.call-done = bf16[1536,768]{1,0:T(8,128)(2,1)} async-done(((bf16[768,768]{1,0:T(8,128)(2,1)}), bf16[1536,768]{1,0:T(8,128)(2,1)}) %all-gather.5.cloned.1.call-update) | async-done | bytes 2359312 | tf_op jit(solution)/shard_map/all_gather | solution.py:120
  60.7 82.6 %while.28 = (s32[]{:T(128)}, bf16[3,512,6,64]{1,3,2,0:T(8,128)(2,1)}, f32[3,6,512]{2,1,0:T(8,128)}, s32[3]{0:T(128)S(1)}, s32[1536,7]{0,1:T(8,128)}, /*index=5*/...) while((s32[]{:T(128)}, ...), condition=%wide.region_5.6_spmd.clone, body=%wide.region_2.5_spmd.clone.sunk | while | flops 1278167552 | bytes 63043776 | solution.py:144
  64.4 6.4 fusion.192
  80.4 7.5 fusion.195
  107.8 7.5 fusion.195
  135.1 7.5 fusion.195
  150.6 34.2 %reduce-scatter.5.cloned.1.call-done = bf16[768,768]{1,0:T(8,128)(2,1)} async-done(((bf16[1536,768]{1,0:T(8,128)(2,1)}), bf16[768,768]{1,0:T(8,128)(2,1)}) %reduce-scatter.5.cloned.1.call-update) | async-done | bytes 1179664 | tf_op jit(solution)/shard_map/reduce_scatter | solution.py:146
  189.3 35.6 %all-gather.7.cloned.1.call-done = bf16[1536,768]{1,0:T(8,128)(2,1)} async-done(((bf16[768,768]{1,0:T(8,128)(2,1)}), bf16[1536,768]{1,0:T(8,128)(2,1)}) %all-gather.7.cloned.1.call-update) | async-done | bytes 2359312 | tf_op jit(solution)/shard_map/all_gather | solution.py:155
  224.9 7.6 fusion.103
  236.9 25.5 %all-gather.9.cloned.1.call-done = bf16[1536,768]{1,0:T(8,128)(2,1)} async-done(((bf16[768,768]{1,0:T(8,128)(2,1)}), bf16[1536,768]{1,0:T(8,128)(2,1)}) %all-gather.9.cloned.1.call-update) | async-done | bytes 2359312 | tf_op jit(solution)/shard_map/all_gather | solution.py:167
  262.5 10.2 %multiply_convert_fusion.1 = (bf16[1536,1024]{1,0:T(8,128)(2,1)S(1)}, bf16[1536,1024]{1,0:T(8,128)(2,1)S(1)}, bf16[1536,1024]{1,0:T(8,128)(2,1)}) fusion(f32[1536,1024]{1,0:T(8,128)} %fusion.102, f32[1536,1024]{1,0:T(8,128)} %fusion.103, bf16[1536,768]{1,0:T(8,128)(2,1)} %all-gather.9.cloned.1.call-done, bf16[1024,768]{1,0:T(8,128)(2,1)S(1)} %copy-done), kind=kOutput, calls=%fused_computation.61 | convolution fusion | flops 2439512064 | bytes 25952256 | tf_op jit(solution)/shard_map/dot_general | solution.py:72
  279.4 34.8 %reduce-scatter.9.cloned.1.call-done = bf16[768,768]{1,0:T(8,128)(2,1)} async-done(((bf16[1536,768]{1,0:T(8,128)(2,1)}), bf16[768,768]{1,0:T(8,128)(2,1)}) %reduce-scatter.9.cloned.1.call-update) | async-done | bytes 1179664 | tf_op jit(solution)/shard_map/reduce_scatter | solution.py:176
  321.9 36.2 %all-gather.11.cloned.1.call-done = bf16[1536,768]{1,0:T(8,128)(2,1)} async-done(((bf16[768,768]{1,0:T(8,128)(2,1)}), bf16[1536,768]{1,0:T(8,128)(2,1)}) %all-gather.11.cloned.1.call-update) | async-done | bytes 2359312 | tf_op jit(solution)/shard_map/all_gather | solution.py:189
  361.8 242.9 %while.29 = (s32[]{:T(128)}, f32[1536,6,64]{0,2,1:T(8,128)}, f32[1536,6,64]{0,2,1:T(8,128)}, f32[3,512,6,64]{1,0,3,2:T(4,128)}, s32[3]{0:T(128)S(1)}, /*index=5*...) while((s32[]{:T(128)}, f32[1536,6,64]{0,2,1:T(8,128)}, ...), condition=%wide.region_13.14_spmd.clone, body=%wide.region_11.13_spmd.clone.sunk | while | flops 3107211776 | bytes 257669424 | solution.py:227
  376.3 6.5 copy-done.1
  382.8 7.7 fusion.210
  390.5 14.7 %multiply_reduce_fusion.3 = (f32[6,512]{1,0:T(8,128)S(1)}, f32[6,512,1536]{2,1,0:T(8,128)}) fusion(f32[6,512,1536]{2,1,0:T(8,128)} %copy-done.1, f32[6,512]{1,0:T(8,128)S(1)} %dynamic-slice_bitcast_fusion.2, pred[512,1536]{1,0:T(8,128)(4,1)S(1)} %fusion.208, bf16[1536,6,64]{0,2,1:T(8,128)(2,1)} %get-tuple-element.502, ...), kind=kOutput, calls=%fused_computation.28.clone.1 | convolution fusion | flops 627569664 | bytes 40132612 | tf_op jit(solution)/shard_map/while/body/eval_jaxpr/qhd,khd->hqk/dot_general | solution.py:206
  405.2 13.2 %multiply_convert_fusion.6 = bf16[6,512,1536]{2,1,0:T(8,128)(2,1)S(1)} fusion(f32[6,512,1536]{2,1,0:T(8,128)} %get-tuple-element.424, f32[6,512,1536]{2,1,0:T(8,128)} %copy-done.1, f32[6,512]{1,0:T(8,128)S(1)} %get-tuple-element.425, f32[6,512]{1,0:T(8,128)S(1)} %dynamic-slice_bitcast_fusion.2, pred[512,1536]{1,0:T(8,128)(4,1)S(1)} %fusion.208), kind=kLoop, calls=%fused_computation.27.clone.1 | loop fusion | flops 28311552 | bytes 47996928 | tf_op jit(solution)/shard_map/while/body/eval_jaxpr/convert_element_type | solution.py:208
  426.7 16.1 %dynamic_update_slice.22 = f32[3,512,6,64]{1,0,3,2:T(4,128)} dynamic-update-slice(f32[3,512,6,64]{1,0,3,2:T(4,128)} %get-tuple-element.480, f32[1,512,6,64]{1,0,3,2:T(1,128)S(1)} %copy.38, s32[]{:T(128)S(6)} %copy.55, s32[]{:T(128)} %constant.41.clone.1..sunk.1, s32[]{:T(128)} %constant.41.clone.1..sunk.1, s32[]{:T(128)} %constant.41.clone.1..sunk.1) | dynamic-update-slice | bytes 1572868 | tf_op jit(solution)/shard_map/while/body/jit(dynamic_update_index_in_dim)/dynamic_update_slice | solution.py:227
  456.8 6.5 copy-done.1
  463.3 8.2 fusion.210
  471.5 14.7 %multiply_reduce_fusion.3 = (f32[6,512]{1,0:T(8,128)S(1)}, f32[6,512,1536]{2,1,0:T(8,128)}) fusion(f32[6,512,1536]{2,1,0:T(8,128)} %copy-done.1, f32[6,512]{1,0:T(8,128)S(1)} %dynamic-slice_bitcast_fusion.2, pred[512,1536]{1,0:T(8,128)(4,1)S(1)} %fusion.208, bf16[1536,6,64]{0,2,1:T(8,128)(2,1)} %get-tuple-element.502, ...), kind=kOutput, calls=%fused_computation.28.clone.1 | convolution fusion | flops 627569664 | bytes 40132612 | tf_op jit(solution)/shard_map/while/body/eval_jaxpr/qhd,khd->hqk/dot_general | solution.py:206
  486.1 13.2 %multiply_convert_fusion.6 = bf16[6,512,1536]{2,1,0:T(8,128)(2,1)S(1)} fusion(f32[6,512,1536]{2,1,0:T(8,128)} %get-tuple-element.424, f32[6,512,1536]{2,1,0:T(8,128)} %copy-done.1, f32[6,512]{1,0:T(8,128)S(1)} %get-tuple-element.425, f32[6,512]{1,0:T(8,128)S(1)} %dynamic-slice_bitcast_fusion.2, pred[512,1536]{1,0:T(8,128)(4,1)S(1)} %fusion.208), kind=kLoop, calls=%fused_computation.27.clone.1 | loop fusion | flops 28311552 | bytes 47996928 | tf_op jit(solution)/shard_map/while/body/eval_jaxpr/convert_element_type | solution.py:208
  507.6 16.1 %dynamic_update_slice.22 = f32[3,512,6,64]{1,0,3,2:T(4,128)} dynamic-update-slice(f32[3,512,6,64]{1,0,3,2:T(4,128)} %get-tuple-element.480, f32[1,512,6,64]{1,0,3,2:T(1,128)S(1)} %copy.38, s32[]{:T(128)S(6)} %copy.55, s32[]{:T(128)} %constant.41.clone.1..sunk.1, s32[]{:T(128)} %constant.41.clone.1..sunk.1, s32[]{:T(128)} %constant.41.clone.1..sunk.1) | dynamic-update-slice | bytes 1572868 | tf_op jit(solution)/shard_map/while/body/jit(dynamic_update_index_in_dim)/dynamic_update_slice | solution.py:227
  537.7 6.5 copy-done.1
  544.2 8.2 fusion.210
  552.3 14.7 %multiply_reduce_fusion.3 = (f32[6,512]{1,0:T(8,128)S(1)}, f32[6,512,1536]{2,1,0:T(8,128)}) fusion(f32[6,512,1536]{2,1,0:T(8,128)} %copy-done.1, f32[6,512]{1,0:T(8,128)S(1)} %dynamic-slice_bitcast_fusion.2, pred[512,1536]{1,0:T(8,128)(4,1)S(1)} %fusion.208, bf16[1536,6,64]{0,2,1:T(8,128)(2,1)} %get-tuple-element.502, ...), kind=kOutput, calls=%fused_computation.28.clone.1 | convolution fusion | flops 627569664 | bytes 40132612 | tf_op jit(solution)/shard_map/while/body/eval_jaxpr/qhd,khd->hqk/dot_general | solution.py:206
  567.0 13.2 %multiply_convert_fusion.6 = bf16[6,512,1536]{2,1,0:T(8,128)(2,1)S(1)} fusion(f32[6,512,1536]{2,1,0:T(8,128)} %get-tuple-element.424, f32[6,512,1536]{2,1,0:T(8,128)} %copy-done.1, f32[6,512]{1,0:T(8,128)S(1)} %get-tuple-element.425, f32[6,512]{1,0:T(8,128)S(1)} %dynamic-slice_bitcast_fusion.2, pred[512,1536]{1,0:T(8,128)(4,1)S(1)} %fusion.208), kind=kLoop, calls=%fused_computation.27.clone.1 | loop fusion | flops 28311552 | bytes 47996928 | tf_op jit(solution)/shard_map/while/body/eval_jaxpr/convert_element_type | solution.py:208
  588.5 16.1 %dynamic_update_slice.22 = f32[3,512,6,64]{1,0,3,2:T(4,128)} dynamic-update-slice(f32[3,512,6,64]{1,0,3,2:T(4,128)} %get-tuple-element.480, f32[1,512,6,64]{1,0,3,2:T(1,128)S(1)} %copy.38, s32[]{:T(128)S(6)} %copy.55, s32[]{:T(128)} %constant.41.clone.1..sunk.1, s32[]{:T(128)} %constant.41.clone.1..sunk.1, s32[]{:T(128)} %constant.41.clone.1..sunk.1) | dynamic-update-slice | bytes 1572868 | tf_op jit(solution)/shard_map/while/body/jit(dynamic_update_index_in_dim)/dynamic_update_slice | solution.py:227
  628.6 7.2 fusion.113
  659.6 33.7 %all-reduce = (f32[768]{0:T(1024)S(1)}, f32[768]{0:T(1024)S(1)}) all-reduce(f32[768]{0:T(1024)S(1)} %get-tuple-element.206, f32[768]{0:T(1024)S(1)} %copy-done.46), channel_id=1, replica_groups=mesh['dp'=16,'mp'=2] {'dp'}, use_global_device_ids=true, to_apply=%region_17.18 | all-reduce | flops 1536 | bytes 12288 | tf_op jit(solution)/shard_map/psum | solution.py:15
  704.0 258.6 %all-reduce.5.cloned.1.call-done = (f32[768,384]{1,0:T(8,128)}, f32[768,384]{1,0:T(8,128)}, f32[768,384]{1,0:T(8,128)}, f32[384,768]{1,0:T(8,128)}, f32[768,1024...) async-done(((f32[768,384]{1,0:T(8,128)}, f32[768,384]{1,0:T(8,128)}, f32[768,384]{1,0:T(8,128)}, f32[384,768]{1,0:T(8,128)}, f32[768,1024]{1,0:T(8,128)}, ...) | async-done | bytes 14155792 | tf_op jit(solution)/shard_map/psum | solution.py:263
  (260 shorter events, 232.8 us)
Async XLA Ops:
  7.2 255.3 %copy-start = (bf16[1024,768]{1,0:T(8,128)(2,1)S(1)}, bf16[1024,768]{1,0:T(8,128)(2,1)}, u32[]{:S(2)}) copy-start(bf16[1024,768]{1,0:T(8,128)(2,1)} %param.26) | copy-start | bytes 4718596
  7.2 45.3 %all-gather.5.cloned.1.call-start = ((), (), s32[]{:S(2)}) async-start(), calls=%async_computation.4 | async-start | bytes 3538944 | tf_op jit(solution)/shard_map/all_gather | solution.py:120
  8.0 6.5 copy-start.57
  10.8 41.6 %copy-start.29 = (bf16[768,384]{1,0:T(8,128)(2,1)S(1)}, bf16[768,384]{1,0:T(8,128)(2,1)}, u32[]{:S(2)}) copy-start(bf16[768,384]{1,0:T(8,128)(2,1)} %param.20) | copy-start | bytes 1769476
  13.5 171.3 %reduce-scatter.5.cloned.1.call-start = ((), (), s32[]{:S(2)}) async-start(), calls=%async_computation.5 | async-start | bytes 3538944 | tf_op jit(solution)/shard_map/reduce_scatter | solution.py:146
  17.2 39.3 %copy-start.18 = (f32[1536,32]{0,1:T(8,128)}, f32[1536,32]{0,1:T(8,128)S(1)}, u32[]{:S(2)}) copy-start(f32[1536,32]{0,1:T(8,128)S(1)} %get-tuple-element.282) | copy-start | bytes 589828
  17.3 39.3 %copy-start.20 = (f32[1536,32]{0,1:T(8,128)}, f32[1536,32]{0,1:T(8,128)S(1)}, u32[]{:S(2)}) copy-start(f32[1536,32]{0,1:T(8,128)S(1)} %get-tuple-element.283) | copy-start | bytes 589828
  17.3 38.1 %copy-start.27 = (bf16[768,384]{1,0:T(8,128)(2,1)S(1)}, bf16[768,384]{1,0:T(8,128)(2,1)}, u32[]{:S(2)}) copy-start(bf16[768,384]{1,0:T(8,128)(2,1)} %param.19) | copy-start | bytes 1769476
  149.9 74.9 %all-gather.7.cloned.1.call-start = ((), (), s32[]{:S(2)}) async-start(), calls=%async_computation.6 | async-start | bytes 3538944 | tf_op jit(solution)/shard_map/all_gather | solution.py:155
  150.6 167.4 %copy-start.33 = (f32[768]{0:T(1024)}, f32[768]{0:T(1024)S(1)}, u32[]{:S(2)}) copy-start(f32[768]{0:T(1024)S(1)} %convert_element_type.122) | copy-start | bytes 9220
  187.1 131.0 %copy-start.35 = (f32[768]{0:T(1024)}, f32[768]{0:T(1024)S(1)}, u32[]{:S(2)}) copy-start(f32[768]{0:T(1024)S(1)} %get-tuple-element.287) | copy-start | bytes 9220
  187.1 130.9 %copy-start.41 = (f32[768]{0:T(1024)}, f32[768]{0:T(1024)S(1)}, u32[]{:S(2)}) copy-start(f32[768]{0:T(1024)S(1)} %get-tuple-element.286) | copy-start | bytes 9220
  188.6 73.8 %all-gather.9.cloned.1.call-start = ((), (), s32[]{:S(2)}) async-start(), calls=%async_computation.8 | async-start | bytes 3538944 | tf_op jit(solution)/shard_map/all_gather | solution.py:167
  189.2 125.0 %reduce-scatter.9.cloned.1.call-start = ((), (), s32[]{:S(2)}) async-start(), calls=%async_computation.9 | async-start | bytes 3538944 | tf_op jit(solution)/shard_map/reduce_scatter | solution.py:176
  224.9 7.6 copy-start.50
  224.9 7.6 copy-start.53
  262.5 10.2 %copy-start.54 = (bf16[768,1024]{1,0:T(8,128)(2,1)S(1)}, bf16[768,1024]{1,0:T(8,128)(2,1)}, u32[]{:S(2)}) copy-start(bf16[768,1024]{1,0:T(8,128)(2,1)} %param.24) | copy-start | bytes 4718596
  279.4 78.7 %all-gather.11.cloned.1.call-start = ((), (), s32[]{:S(2)}) async-start(), calls=%async_computation.10 | async-start | bytes 3538944 | tf_op jit(solution)/shard_map/all_gather | solution.py:189
  321.8 335.4 %reduce-scatter.11.cloned.1.call-start = ((), (), s32[]{:S(2)}) async-start(), calls=%async_computation.11 | async-start | bytes 3538944 | tf_op jit(solution)/shard_map/reduce_scatter | solution.py:245
  376.3 6.5 copy-start.1
  456.8 6.5 copy-start.1
  537.7 6.5 copy-start.1
  611.5 7.9 copy-start.13
  622.3 76.5 %reduce-scatter.7.cloned.1.call-start = ((), (), s32[]{:S(2)}) async-start(), calls=%async_computation.7 | async-start | bytes 3538944 | tf_op jit(solution)/shard_map/reduce_scatter | solution.py:161
  628.3 334.3 %all-reduce.5.cloned.1.call-start = ((), (), s32[]{:S(2)}) async-start(), calls=%async_computation.12 | async-start | bytes 28311552 | tf_op jit(solution)/shard_map/psum | solution.py:263
  628.6 7.2 copy-start.51
  628.6 7.2 copy-start.62
  654.1 44.8 %copy-start.34 = (f32[768]{0:T(1024)S(1)}, f32[768]{0:T(1024)}, u32[]{:S(2)}) copy-start(f32[768]{0:T(1024)} %copy-done.33) | copy-start | bytes 9220
  654.1 44.8 %copy-start.36 = (f32[768]{0:T(1024)S(1)}, f32[768]{0:T(1024)}, u32[]{:S(2)}) copy-start(f32[768]{0:T(1024)} %copy-done.35) | copy-start | bytes 9220
  654.1 44.8 %copy-start.42 = (f32[768]{0:T(1024)S(1)}, f32[768]{0:T(1024)}, u32[]{:S(2)}) copy-start(f32[768]{0:T(1024)} %copy-done.41) | copy-start | bytes 9220
  654.1 44.8 %copy-start.44 = (f32[768]{0:T(1024)S(1)}, f32[768]{0:T(1024)}, u32[]{:S(2)}) copy-start(f32[768]{0:T(1024)} %copy-done.43) | copy-start | bytes 9220
  654.1 44.8 %copy-start.45 = (f32[768]{0:T(1024)S(1)}, f32[768]{0:T(1024)}, u32[]{:S(2)}) copy-start(f32[768]{0:T(1024)} %get-tuple-element.284) | copy-start | bytes 9220
  (46 other events, 122.8 us)
Sparse Core Ops, SparseCore 0:
  13.7 38.7 all-gather.4
  150.1 34.7 reduce-scatter.4
  188.7 36.0 all-gather.6
  226.3 36.0 all-gather.8
  279.5 34.6 reduce-scatter.8
  321.9 36.0 all-gather.10
  622.5 34.7 reduce-scatter.10
  660.1 34.7 reduce-scatter.6
  701.5 261.0 all-reduce.4
